TPU v7x, 32 devices: a whole 2x2x4 slice. The times are simulated.
32 devices in a mesh: row: 4 (over y, core), col: 8 (over z, x).
Axes of the slice: x: 2, y: 2, z: 4, core: 2. Of those that a mesh axis runs over, the one named last changes fastest.
Arguments:
- front: float32 [12288, 12288], P('row', 'col'), may hold values from -6 to 6
- delayed: float32 [64, 12288], P('col', 'row'), may hold values from -6 to 6
- dest: int32 [64], P('col'), may hold values from 0 to 1023, as said below
- pivots: int32 [1024], replicated, may hold values from 0 to 12287, as said below
- pair_flags: int32 [1024], replicated, may hold values from 0 to 1, as said below
- linv: float32 [4, 256, 256], replicated, as said below
- dinv_diag: float32 [1024], replicated, may hold values from -0.1 to 0.1
- dinv_off: float32 [1024], replicated, may hold values from -0.08 to 0.08
Outputs:
- trailing: float32 [12288, 12288], P('row', 'col')
- factor: float32 [12288, 1024], P('row')
Inputs may be any that keep to these rules, and one draw needn't show every extreme that they name: Distinct front columns; slots p * 256 to (p + 1) * 256 - 1 are panel p's pivots. Each block of 1536 columns held by one index of col contains exactly 128 of them. `pair_flags`: A 1 at slot s joins slots s and s + 1 into one 2x2 block; no two 1s are adjacent and the last slot of a panel holds 0. `dest`: several delayed columns may share a slot. Of the 8 delayed columns held by one index of col, at most 2 go to pivot columns held by the same index of col. `linv`: each panel's matrix is unit lower triangular: ones on the diagonal, zeros above it.
All inputs are finite; a program needn't handle non-finite values.
Results may differ from a plain program's by a relative error of at most 0.00015.
Values sent between devices are 32-bit elements; how exact they have to be, the bound alone decides.
A program may use at most 192 MiB of HBM per device.

v0:
```python
import jax
import jax.numpy as jnp
from jax import lax
from jax.sharding import PartitionSpec as P

CAP = 2
precise = lax.Precision.HIGHEST


def broadcast(block, axis, holder):
    block = jnp.where(lax.axis_index(axis) == holder, block, jnp.zeros_like(block))
    return lax.psum(block, axis)


def pair_scale(scaled, pair_bits, diag_part, off_part):
    coupled = pair_bits.astype(jnp.float32) * off_part
    zero_col = jnp.zeros_like(scaled[:, :1])
    shifted_next = jnp.concatenate([scaled[:, 1:], zero_col], axis=1)
    shifted_prev = jnp.concatenate([zero_col, scaled[:, :-1]], axis=1)
    coupled_prev = jnp.concatenate([jnp.zeros_like(coupled[:1]), coupled[:-1]])
    return scaled * diag_part + shifted_next * coupled + shifted_prev * coupled_prev


def select_columns(matrix, wanted, anchor):
    block_width = matrix.shape[1]
    relative = wanted - anchor
    inside = (relative >= 0) & (relative < block_width)
    clipped = jnp.clip(relative, 0, block_width - 1)
    return jnp.where(inside[None, :], jnp.take(matrix, clipped, axis=1), 0.0)


def select_rows(matrix, wanted, anchor):
    block_height = matrix.shape[0]
    relative = wanted - anchor
    inside = (relative >= 0) & (relative < block_height)
    clipped = jnp.clip(relative, 0, block_height - 1)
    return jnp.where(inside[:, None], jnp.take(matrix, clipped, axis=0), 0.0)


def body(front, delayed, dest, pivots, pair_flags, linv, dinv_diag, dinv_off):
    col_count = lax.axis_size("col")
    rows_blk, cols_blk = front.shape
    row_start = lax.axis_index("row") * rows_blk
    col_start = lax.axis_index("col") * cols_blk
    panel_count = linv.shape[0]
    panel_width = linv.shape[1]
    slot_total = pivots.shape[0]
    slot_ids = jnp.arange(slot_total, dtype=jnp.int32)
    owner_ids = jnp.arange(col_count, dtype=jnp.int32)
    slot_hit = dest[:, None] == slot_ids[None, :]
    targets = jnp.sum(jnp.where(slot_hit, pivots[None, :], 0), axis=1)
    owners = targets // cols_blk
    within = targets - owners * cols_blk
    owner_hit = (owners[:, None] == owner_ids[None, :]).astype(jnp.int32)
    earlier = jnp.cumsum(owner_hit, axis=0) - owner_hit
    rank_in = jnp.sum(earlier * owner_hit, axis=1)
    slot_pos = jnp.arange(CAP, dtype=jnp.int32)
    placed = (owner_hit[:, :, None] > 0) & (rank_in[:, None, None] == slot_pos[None, None, :])
    send_vals = jnp.einsum("kos,kr->osr", placed.astype(jnp.float32), delayed, precision=precise)
    send_cols = jnp.sum(jnp.where(placed, within[:, None, None] + 1, 0), axis=0) - 1
    recv_vals, recv_cols = (
        lax.all_to_all(send_vals, "col", split_axis=0, concat_axis=0, tiled=True),
        lax.all_to_all(send_cols, "col", split_axis=0, concat_axis=0, tiled=True),
    )
    flat_vals = recv_vals.reshape(-1, rows_blk)
    flat_cols = recv_cols.reshape(-1)
    col_ids = jnp.arange(cols_blk, dtype=jnp.int32)
    col_hit = (flat_cols[:, None] == col_ids[None, :]).astype(jnp.float32)
    current = front + lax.dot_general(
        flat_vals, col_hit, (((0,), (0,)), ((), ())), precision=precise
    )
    factors = []
    piv_owner = pivots // cols_blk
    piv_hit = (piv_owner[:, None] == owner_ids[None, :]).astype(jnp.int32)
    piv_rank = jnp.sum((jnp.cumsum(piv_hit, axis=0) - piv_hit) * piv_hit, axis=1)
    per_owner = slot_total // col_count
    owned_here = piv_owner == lax.axis_index("col")
    rank_ids = jnp.arange(per_owner, dtype=jnp.int32)
    own_slots = jnp.sum(
        jnp.where(
            owned_here[None, :] & (piv_rank[None, :] == rank_ids[:, None]), slot_ids[None, :], 0
        ),
        axis=1,
    )
    compact = select_columns(current, pivots[own_slots], col_start)
    gathered = lax.all_gather(compact, "col", axis=1, tiled=True)
    every_panel = jnp.take(gathered, piv_owner * per_owner + piv_rank, axis=1)
    previous = []
    for panel_index in range(panel_count):
        offset = panel_index * panel_width
        panel_cols = every_panel[:, offset : offset + panel_width]
        for cols_before, rows_before in previous:
            panel_cols = panel_cols - lax.dot_general(
                cols_before,
                rows_before[offset : offset + panel_width],
                (((1,), (1,)), ((), ())),
                precision=precise,
            )
        finish_offset = panel_index * panel_width
        finish_scaled = jnp.dot(panel_cols, jnp.transpose(linv[panel_index]), precision=precise)
        finish_columns = pair_scale(
            finish_scaled,
            pair_flags[finish_offset : finish_offset + panel_width],
            dinv_diag[finish_offset : finish_offset + panel_width],
            dinv_off[finish_offset : finish_offset + panel_width],
        )
        root_row = col_start // rows_blk
        slice_start = jnp.clip(col_start - row_start, 0, rows_blk - cols_blk)
        root_piece = lax.dynamic_slice_in_dim(finish_scaled, slice_start, cols_blk, 0)
        col_scaled = broadcast(root_piece, "row", root_row)
        current = current - lax.dot_general(
            finish_columns, col_scaled, (((1,), (1,)), ((), ())), precision=precise
        )
        factors.append(finish_columns)
        if panel_index + 1 < panel_count:
            pivot_part = select_rows(finish_scaled, pivots, row_start)
            pivot_rows = lax.psum(pivot_part, "row")
            previous.append((finish_columns, pivot_rows))
    row_ids = row_start + jnp.arange(rows_blk, dtype=jnp.int32)
    row_in = jnp.any(row_ids[:, None] == pivots[None, :], axis=1)
    col_in = jnp.any((col_start + col_ids)[:, None] == pivots[None, :], axis=1)
    trailing = jnp.where(row_in[:, None] | col_in[None, :], 0.0, current)
    factor = jnp.concatenate(factors, axis=1)
    return (trailing, factor)


def solution(mesh):
    return jax.shard_map(
        body,
        mesh=mesh,
        in_specs=(P("row", "col"), P("col", "row"), P("col"), P(), P(), P(), P(), P()),
        out_specs=(P("row", "col"), P("row", None)),
        check_vma=False,
    )
```

profile of v0, /device:TPU:0, one launch (start us, length us, event | category | flops | bytes accessed | tf_op | source)
XLA Modules:
  0.0 721.7 jit_solution(9475887452106300543)
XLA Ops:
  9.2 7.3 %all-to-all-start.1 = ((s32[8,1,2]{2,1,0:T(1,128)}), s32[8,1,2]{2,1,0:T(1,128)S(1)}, u32[]{:S(2)}, u32[]{:S(2)}) async-start(s32[8,1,2]{2,1,0:T(1,128)} %copy.32), calls=%async_computation.1 | async-start | bytes 8192 | tf_op jit(solution)/shard_map/all_to_all | solution.py:63
  18.2 2.3 reduce-window.6
  22.9 6.0 all-to-all-start
  30.2 6.4 all-to-all-done
  36.8 18.0 %convolution_add_fusion = f32[3072,1536]{1,0:T(8,128)} fusion(f32[3072,1536]{1,0:T(8,128)} %param.10, f32[16,3072]{1,0:T(8,128)S(1)} %reshape.189, s32[16]{0:T(128)S(1)} %eq.152), kind=kOutput, calls=%fused_computation.7 | convolution fusion | flops 910712832 | bytes 37945408 | tf_op jit(solution)/shard_map/dot_general | solution.py:69
  54.8 18.7 %copy.33 = f32[3072,1536]{0,1:T(8,128)} copy(f32[3072,1536]{1,0:T(8,128)} %convolution_add_fusion) | data formatting | bytes 37748736 | tf_op jit(solution)/shard_map/add | solution.py:69
  73.4 8.2 %gather_fusion.1 = f32[128,3072]{1,0:T(8,128)S(1)} fusion(f32[3072,1536]{0,1:T(8,128)} %copy.33, s32[1024]{0:T(1024)S(1)} %pad_clamp_fusion), kind=kCustom, calls=%fused_computation.4 | custom fusion | bytes 3146240 | tf_op jit(solution)/shard_map/jit(_take)/gather | solution.py:29
  84.1 173.5 %all-gather.2.cloned.1.call-done = f32[3072,1024]{0,1:T(8,128)} async-done(((f32[3072,128]{0,1:T(8,128)}), f32[3072,1024]{0,1:T(8,128)}) %all-gather.2.cloned.1.call-update) | async-done | bytes 12582928 | tf_op jit(solution)/shard_map/all_gather | solution.py:86
  257.6 16.5 %gather_fusion.2 = f32[1024,3072]{1,0:T(8,128)} fusion(f32[3072,1024]{0,1:T(8,128)} %all-gather.2.cloned.1.call-done, s32[1024]{0:T(1024)S(1)} %broadcast_clamp_fusion), kind=kCustom, calls=%fused_computation.5 | custom fusion | bytes 25169920 | tf_op jit(solution)/shard_map/jit(_take)/gather | solution.py:87
  274.1 12.6 %copy.34 = f32[1024,3072]{0,1:T(8,128)} copy(f32[1024,3072]{1,0:T(8,128)} %gather_fusion.2) | data formatting | bytes 25165824 | tf_op jit(solution)/shard_map/jit(_take)/gather | solution.py:87
  286.7 12.4 %select_bitcast_fusion = f32[3072,1024]{1,0:T(8,128)} fusion(f32[1024,3072]{0,1:T(8,128)} %copy.34, pred[1024]{0:T(1024)(128)(4,1)S(1)} %compare_and_fusion.2), kind=kLoop, calls=%fused_computation.9 | loop fusion | flops 3145728 | bytes 25166848 | tf_op jit(solution)/shard_map/jit(_take)/select_n | solution.py:87
  299.1 4.8 fusion
  304.0 3.7 fusion.40
  307.7 2.3 copy.35
  310.0 5.3 gather_fusion.3
  316.9 5.3 multiply_add_fusion.3
  324.0 27.4 %all-reduce.14.cloned.1.call-done = f32[1024,256]{1,0:T(8,128)} async-done(((f32[1024,256]{1,0:T(8,128)}), f32[1024,256]{1,0:T(8,128)}) %all-reduce.14.cloned.1.call-update) | async-done | bytes 1048592 | tf_op jit(solution)/shard_map/psum | solution.py:117
  351.4 7.3 %convolution_subtract_fusion.5 = f32[3072,256]{1,0:T(8,128)S(1)} fusion(f32[3072,256]{0,1:T(8,128)S(1)} %multiply_add_fusion.3, f32[3072,1024]{1,0:T(8,128)} %select_bitcast_fusion, f32[1024,256]{1,0:T(8,128)} %all-reduce.14.cloned.1.call-done), kind=kOutput, calls=%fused_computation.17 | convolution fusion | flops 2416705536 | bytes 9699328 | tf_op jit(solution)/shard_map/dot_general | solution.py:93
  358.7 4.1 fusion.13
  364.4 3.3 fusion.39
  367.8 3.5 copy.36
  371.3 6.6 gather_fusion.4
  377.8 2.5 select_select_fusion.1
  380.7 7.0 multiply_add_fusion.2
  387.6 8.0 %convolution_subtract_fusion.4 = f32[3072,256]{1,0:T(8,128)} fusion(f32[3072,256]{0,1:T(8,128)S(1)} %multiply_add_fusion.3, f32[3072,1024]{1,0:T(8,128)} %select_bitcast_fusion, f32[1024,256]{1,0:T(8,128)S(1)} %copy-done.19), kind=kOutput, calls=%fused_computation.16 | convolution fusion | flops 2416705536 | bytes 9699328 | tf_op jit(solution)/shard_map/dot_general | solution.py:93
  397.3 8.3 %convolution_subtract_fusion.2 = f32[3072,256]{1,0:T(8,128)} fusion(f32[3072,256]{0,1:T(8,128)S(1)} %multiply_add_fusion.3, f32[3072,1024]{1,0:T(8,128)} %select_bitcast_fusion, f32[1024,256]{1,0:T(8,128)S(1)} %copy-done.19), kind=kOutput, calls=%fused_computation.14 | convolution fusion | flops 2416705536 | bytes 9699328 | tf_op jit(solution)/shard_map/dot_general | solution.py:93
  405.5 11.8 %all-reduce.16.cloned.1.call-done = f32[1024,256]{1,0:T(8,128)} async-done(((f32[1024,256]{1,0:T(8,128)}), f32[1024,256]{1,0:T(8,128)}) %all-reduce.16.cloned.1.call-update) | async-done | bytes 1048592 | tf_op jit(solution)/shard_map/psum | solution.py:117
  417.3 8.3 %convolution_subtract_fusion.3 = f32[3072,256]{1,0:T(8,128)S(1)} fusion(f32[3072,256]{1,0:T(8,128)} %convolution_subtract_fusion.4, f32[3072,256]{0,1:T(8,128)} %multiply_add_fusion.2, f32[1024,256]{1,0:T(8,128)} %all-reduce.16.cloned.1.call-done), kind=kOutput, calls=%fused_computation.15 | convolution fusion | flops 2416705536 | bytes 9699328 | tf_op jit(solution)/shard_map/dot_general | solution.py:93
  425.7 4.1 fusion.11
  429.8 1.7 copy-done.2
  431.4 3.3 fusion.38
  434.7 3.5 copy.37
  438.2 6.6 gather_fusion.5
  444.8 2.6 select_select_fusion
  447.7 7.0 multiply_add_fusion.1
  457.2 8.1 %convolution_subtract_fusion.1 = f32[3072,256]{1,0:T(8,128)} fusion(f32[3072,256]{1,0:T(8,128)S(1)} %copy-done.16, f32[3072,256]{0,1:T(8,128)S(1)} %copy-done.8, f32[1024,256]{1,0:T(8,128)} %all-reduce.16.cloned.1.call-done), kind=kOutput, calls=%fused_computation.13 | convolution fusion | flops 2416705536 | bytes 9699328 | tf_op jit(solution)/shard_map/dot_general | solution.py:93
  465.3 19.0 %all-reduce.18.cloned.1.call-done = f32[1024,256]{1,0:T(8,128)} async-done(((f32[1024,256]{1,0:T(8,128)}), f32[1024,256]{1,0:T(8,128)}) %all-reduce.18.cloned.1.call-update) | async-done | bytes 1048592 | tf_op jit(solution)/shard_map/psum | solution.py:117
  484.4 8.3 %convolution_subtract_fusion = f32[3072,256]{1,0:T(8,128)S(1)} fusion(f32[3072,256]{1,0:T(8,128)} %convolution_subtract_fusion.1, f32[3072,256]{0,1:T(8,128)} %multiply_add_fusion.1, f32[1024,256]{1,0:T(8,128)} %all-reduce.18.cloned.1.call-done), kind=kOutput, calls=%fused_computation.12 | convolution fusion | flops 2416705536 | bytes 9699328 | tf_op jit(solution)/shard_map/dot_general | solution.py:93
  492.7 4.3 fusion.9
  501.4 2.0 compare_reduce_fusion
  503.4 3.9 fusion.37
  512.0 5.4 pad_maximum_fusion
  517.4 12.6 %copy.38 = f32[3072,1024]{1,0:T(8,128)} copy(f32[3072,1024]{0,1:T(8,128)} %pad_maximum_fusion) | data formatting | bytes 25165824
  530.0 90.6 %all-reduce.20.cloned.1.call-done = (f32[1536,256]{0,1:T(8,128)}, f32[1536,256]{0,1:T(8,128)}, f32[1536,256]{0,1:T(8,128)}, f32[1536,256]{0,1:T(8,128)}) async-done(((f32[1536,256]{0,1:T(8,128)}, f32[1536,256]{0,1:T(8,128)}, f32[1536,256]{0,1:T(8,128)}, f32[1536,256]{0,1:T(8,128)}), (f32[1536,256]{0,1:T(8,128)}, f32[1536,256]{0,1:T(8,128)}, f32[1536,256]{0,1:T(8,128)}, ...) | async-done | bytes 6291472 | tf_op jit(solution)/shard_map/psum | solution.py:12
  620.6 19.9 %fusion.44 = f32[3072,1536]{1,0:T(8,128)} fusion(f32[3072,256]{0,1:T(8,128)} %multiply_add_fusion.1, f32[1536,256]{0,1:T(8,128)} %get-tuple-element.11), kind=kOutput, calls=%fused_computation.119 | convolution fusion | flops 14495514624 | bytes 23592960 | tf_op jit(solution)/shard_map/dot_general | solution.py:111
  640.5 18.5 %fusion.43 = f32[3072,1536]{1,0:T(8,128)} fusion(f32[3072,256]{0,1:T(8,128)S(1)} %copy-done.10, f32[1536,256]{0,1:T(8,128)S(1)} %copy-done.18), kind=kOutput, calls=%fused_computation.118 | convolution fusion | flops 14495514624 | bytes 23592960 | tf_op jit(solution)/shard_map/dot_general | solution.py:111
  659.0 17.9 %fusion.42 = f32[3072,1536]{1,0:T(8,128)} fusion(f32[3072,256]{0,1:T(8,128)S(1)} %multiply_add_fusion.3, f32[1536,256]{0,1:T(8,128)S(1)} %copy-done.17), kind=kOutput, calls=%fused_computation.117 | convolution fusion | flops 14495514624 | bytes 23592960 | tf_op jit(solution)/shard_map/dot_general | solution.py:111
  676.9 38.1 %subtract_select_fusion = f32[3072,1536]{1,0:T(8,128)} fusion(f32[3072,1536]{1,0:T(8,128)} %fusion.44, f32[3072,1536]{1,0:T(8,128)} %fusion.43, f32[3072,1536]{1,0:T(8,128)} %convolution_add_fusion, f32[3072,1536]{1,0:T(8,128)} %fusion.42, f32[3072,256]{0,1:T(8,128)} %copy-done.15, f32[1536,256]{0,1:T(8,128)} %get-tuple-element.14, ...), kind=kOutput, calls=%fused_computation.6 | convolution fusion | flops 14523826176 | bytes 99095040 | tf_op jit(solution)/shard_map/dot_general | solution.py:111
  (102 shorter events, 28.4 us)
Async XLA Ops:
  7.2 9.3 %copy-start = (f32[8,3072]{1,0:T(8,128)S(1)}, f32[8,3072]{1,0:T(8,128)}, u32[]{:S(2)}) copy-start(f32[8,3072]{1,0:T(8,128)} %param.11) | copy-start | bytes 294916
  9.2 13.7 %all-to-all-start.1 = ((s32[8,1,2]{2,1,0:T(1,128)}), s32[8,1,2]{2,1,0:T(1,128)S(1)}, u32[]{:S(2)}, u32[]{:S(2)}) async-start(s32[8,1,2]{2,1,0:T(1,128)} %copy.32), calls=%async_computation.1 | async-start | bytes 8192 | tf_op jit(solution)/shard_map/all_to_all | solution.py:63
  22.9 13.8 %all-to-all-start = ((f32[8,2,3072]{2,1,0:T(2,128)}), f32[8,2,3072]{2,1,0:T(2,128)S(1)}, u32[]{:S(2)}, u32[]{:S(2)}) async-start(f32[8,2,3072]{2,1,0:T(2,128)} %copy.31), calls=%async_computation | async-start | bytes 393216 | tf_op jit(solution)/shard_map/all_to_all | solution.py:62
  28.9 228.7 %all-gather.2.cloned.1.call-start = ((), (), s32[]{:S(2)}) async-start(), calls=%async_computation.2 | async-start | bytes 14155776 | tf_op jit(solution)/shard_map/all_gather | solution.py:86
  81.7 2.1 copy-start.20
  81.7 2.1 copy-start.21
  81.7 2.3 copy-start.11
  81.7 2.3 copy-start.22
  83.2 268.2 %all-reduce.14.cloned.1.call-start = ((), (), s32[]{:S(2)}) async-start(), calls=%async_computation.3 | async-start | bytes 2097152 | tf_op jit(solution)/shard_map/psum | solution.py:117
  304.0 3.7 copy-start.6
  316.7 100.6 %all-reduce.16.cloned.1.call-start = ((), (), s32[]{:S(2)}) async-start(), calls=%async_computation.4 | async-start | bytes 2097152 | tf_op jit(solution)/shard_map/psum | solution.py:117
  316.9 5.4 copy-start.7
  362.8 1.7 copy-start.4
  380.4 103.9 %all-reduce.18.cloned.1.call-start = ((), (), s32[]{:S(2)}) async-start(), calls=%async_computation.5 | async-start | bytes 2097152 | tf_op jit(solution)/shard_map/psum | solution.py:117
  380.7 7.0 copy-start.19
  387.6 8.0 %copy-start.5 = (f32[3072,256]{0,1:T(8,128)S(1)}, f32[3072,256]{0,1:T(8,128)}, u32[]{:S(2)}) copy-start(f32[3072,256]{0,1:T(8,128)} %copy-done.4) | copy-start | bytes 9437188
  429.7 1.7 copy-start.2
  447.5 173.2 %all-reduce.20.cloned.1.call-start = ((), (), s32[]{:S(2)}) async-start(), calls=%async_computation.6 | async-start | bytes 12582912 | tf_op jit(solution)/shard_map/psum | solution.py:12
  447.7 7.1 copy-start.3
  447.7 8.7 %copy-start.16 = (f32[3072,256]{1,0:T(8,128)S(1)}, f32[3072,256]{1,0:T(8,128)}, u32[]{:S(2)}) copy-start(f32[3072,256]{1,0:T(8,128)} %convolution_subtract_fusion.2) | copy-start | bytes 9437188
  454.7 2.5 copy-start.8
  497.0 1.7 copy-start.12
  503.4 4.6 copy-start.13
  508.0 3.0 copy-start.9
  508.0 4.0 copy-start.14
  509.3 1.7 copy-start.15
  620.6 19.9 %copy-start.10 = (f32[3072,256]{0,1:T(8,128)S(1)}, f32[3072,256]{0,1:T(8,128)}, u32[]{:S(2)}) copy-start(f32[3072,256]{0,1:T(8,128)} %multiply_add_fusion.2) | copy-start | bytes 9437188
  620.6 19.9 %copy-start.18 = (f32[1536,256]{0,1:T(8,128)S(1)}, f32[1536,256]{0,1:T(8,128)}, u32[]{:S(2)}) copy-start(f32[1536,256]{0,1:T(8,128)} %get-tuple-element.12) | copy-start | bytes 4718596
  640.5 18.5 %copy-start.17 = (f32[1536,256]{0,1:T(8,128)S(1)}, f32[1536,256]{0,1:T(8,128)}, u32[]{:S(2)}) copy-start(f32[1536,256]{0,1:T(8,128)} %get-tuple-element.13) | copy-start | bytes 4718596
  676.9 38.1 %copy-start.1 = (f32[8,3072]{1,0:T(8,128)S(1)}, f32[8,3072]{1,0:T(8,128)}, u32[]{:S(2)}) copy-start(f32[8,3072]{1,0:T(8,128)} %param.11) | copy-start | bytes 294916
Sparse Core Ops, SparseCore 0:
  83.3 174.2 all-gather.1
  316.8 34.4 all-reduce.13
  380.5 36.7 all-reduce.15
  447.6 36.7 all-reduce.17
  500.5 120.0 all-reduce.19
where the time goes:
time: 728 us; the launch traced here: 722 us
  waiting for transfers between devices  329 us (45%)
  matrix products  178 us (24%)
  local copies, waits for them, and re-layouts  124 us (17%)
  other arithmetic  61.7 us (8%)
  starting transfers between devices  14.6 us (2%)
  between operations  14.4 us (2%)
    all_gather x1, waiting for transfers between devices, body(): gathered = lax.all_gather(compact, 'col', axis=1, tiled=True)  174 us
    dot_general x4, matrix products, body(): lax.dot_general(finish_columns, col_scaled, (((1,), (1,)), ((), ())), pre...  94.3 us
    psum x1, waiting for transfers between devices, broadcast(): return lax.psum(block, axis)  90.6 us
    psum x3, waiting for transfers between devices, body(): pivot_rows = lax.psum(pivot_part, 'row')  58.2 us
    dot_general x6, matrix products, body(): lax.dot_general(cols_before, rows_before[offset:offset + panel_width], ((...  48.4 us
    gather x2, local copies, waits for them, and re-layouts, body(): every_panel = jnp.take(gathered, piv_owner * per_owner + piv_rank, axis=1)  29.1 us
    unnamed x47, local copies, waits for them, and re-layouts  21.9 us
    add x4, other arithmetic, pair_scale(): scaled * diag_part + shifted_next * coupled + shifted_prev * coupled_prev  20.7 us
  transfers between devices with their start and end apart: 7, of which 6 were waited for; matrix products, arithmetic and copies ran while one was open for 11% of the time, Pallas kernels for 0%

commit v1 on v0

--- a/solution.py
+++ b/solution.py
@@ -83,7 +83,14 @@
         axis=1,
     )
     compact = select_columns(current, pivots[own_slots], col_start)
-    gathered = lax.all_gather(compact, "col", axis=1, tiled=True)
+    size = lax.axis_size("col")
+    route = [(i, (i + 1) % size) for i in range(size)]
+    parts = [compact]
+    for far in range(1, size):
+        parts = [lax.ppermute(parts[0], "col", route), *parts]
+    out = jnp.concatenate(parts, axis=1)
+    shift = (lax.axis_index("col") + 1) * parts[-1].shape[1]
+    gathered = jnp.roll(out, shift, axis=1)
     every_panel = jnp.take(gathered, piv_owner * per_owner + piv_rank, axis=1)
     previous = []
     for panel_index in range(panel_count):

time: 728 us -> 837 us (1.15)
  waiting for transfers between devices: 329 us -> 393 us
  local copies, waits for them, and re-layouts: 124 us -> 165 us
    ppermute x0 -> x7, waiting for transfers between devices: none -> 241 us  [body(): parts = [lax.ppermute(parts[0], 'col', route), *parts]]
    all_gather x1 -> x0, waiting for transfers between devices: 174 us -> none  [body(): gathered = lax.all_gather(compact, 'col', axis=1, tiled=True)]
    unnamed x47 -> x77, local copies, waits for them, and re-layouts: 21.9 us -> 50.9 us
    dynamic_slice x0 -> x1, local copies, waits for them, and re-layouts: none -> 11 us  [body(): gathered = jnp.roll(out, shift, axis=1)]
  transfers between devices with their start and end apart: 7 -> 13, of which waited for: 6 -> 12; matrix products, arithmetic and copies ran while one was open for 11% -> 10% of each run, Pallas kernels for 0% -> 0%
where the time goes in v1:
time: 837 us; the launch traced here: 830 us
  waiting for transfers between devices  393 us (47%)
  matrix products  178 us (21%)
  local copies, waits for them, and re-layouts  165 us (20%)
  other arithmetic  64 us (8%)
  starting transfers between devices  15.4 us (2%)
  between operations  14.4 us (2%)
    ppermute x7, waiting for transfers between devices, body(): parts = [lax.ppermute(parts[0], 'col', route), *parts]  241 us
    dot_general x4, matrix products, body(): lax.dot_general(finish_columns, col_scaled, (((1,), (1,)), ((), ())), pre...  94.2 us
    psum x1, waiting for transfers between devices, broadcast(): return lax.psum(block, axis)  89.8 us
    psum x3, waiting for transfers between devices, body(): pivot_rows = lax.psum(pivot_part, 'row')  57.2 us
    unnamed x77, local copies, waits for them, and re-layouts  50.9 us
    dot_general x6, matrix products, body(): lax.dot_general(cols_before, rows_before[offset:offset + panel_width], ((...  48.1 us
    gather x2, local copies, waits for them, and re-layouts, body(): every_panel = jnp.take(gathered, piv_owner * per_owner + piv_rank, axis=1)  29.2 us
    add x4, other arithmetic, pair_scale(): scaled * diag_part + shifted_next * coupled + shifted_prev * coupled_prev  20.7 us
  transfers between devices with their start and end apart: 13, of which 12 were waited for; matrix products, arithmetic and copies ran while one was open for 10% of the time, Pallas kernels for 0%

profile of v1, /device:TPU:0, one launch (start us, length us, event | category | flops | bytes accessed | tf_op | source)
XLA Modules:
  0.0 830.0 jit_solution(8060164370416268573)
XLA Ops:
  9.2 7.3 all-to-all-start.1
  22.9 6.0 all-to-all-start
  30.9 5.8 all-to-all-done
  36.8 18.0 %convolution_add_fusion = f32[3072,1536]{1,0:T(8,128)} fusion(f32[3072,1536]{1,0:T(8,128)} %param.10, f32[16,3072]{1,0:T(8,128)S(1)} %reshape.189, s32[16]{0:T(128)S(1)} %eq.155), kind=kOutput, calls=%fused_computation.7 | convolution fusion | flops 910712832 | bytes 37945408 | tf_op jit(solution)/shard_map/dot_general | solution.py:69
  54.8 18.7 %copy.33 = f32[3072,1536]{0,1:T(8,128)} copy(f32[3072,1536]{1,0:T(8,128)} %convolution_add_fusion) | data formatting | bytes 37748736 | tf_op jit(solution)/shard_map/add | solution.py:69
  73.4 8.2 gather_fusion.1
  83.0 35.9 %collective-permute-done = f32[3072,128]{0,1:T(8,128)S(1)} collective-permute-done((f32[3072,128]{0,1:T(8,128)S(1)}, f32[3072,128]{0,1:T(8,128)S(1)}, u32[]{:S(2)}, u32[]{:S(2)}) %collective-permute-start) | collective-permute-done | bytes 1572896 | tf_op jit(solution)/shard_map/ppermute | solution.py:90
  118.9 36.0 %collective-permute-done.1 = f32[3072,128]{0,1:T(8,128)S(1)} collective-permute-done((f32[3072,128]{0,1:T(8,128)S(1)}, f32[3072,128]{0,1:T(8,128)S(1)}, u32[]{:S(2)}, u32[]{:S(2)}) %collective-permute-start.1) | collective-permute-done | bytes 1572896 | tf_op jit(solution)/shard_map/ppermute | solution.py:90
  156.1 35.1 %collective-permute-done.2 = f32[3072,128]{0,1:T(8,128)S(1)} collective-permute-done((f32[3072,128]{0,1:T(8,128)S(1)}, f32[3072,128]{0,1:T(8,128)S(1)}, u32[]{:S(2)}, u32[]{:S(2)}) %collective-permute-start.2) | collective-permute-done | bytes 1572896 | tf_op jit(solution)/shard_map/ppermute | solution.py:90
  192.4 34.3 %collective-permute-done.3 = f32[3072,128]{0,1:T(8,128)S(1)} collective-permute-done((f32[3072,128]{0,1:T(8,128)S(1)}, f32[3072,128]{0,1:T(8,128)S(1)}, u32[]{:S(2)}, u32[]{:S(2)}) %collective-permute-start.3) | collective-permute-done | bytes 1572896 | tf_op jit(solution)/shard_map/ppermute | solution.py:90
  227.8 33.4 %collective-permute-done.4 = f32[3072,128]{0,1:T(8,128)S(1)} collective-permute-done((f32[3072,128]{0,1:T(8,128)S(1)}, f32[3072,128]{0,1:T(8,128)S(1)}, u32[]{:S(2)}, u32[]{:S(2)}) %collective-permute-start.4) | collective-permute-done | bytes 1572896 | tf_op jit(solution)/shard_map/ppermute | solution.py:90
  262.3 34.2 %collective-permute-done.5 = f32[3072,128]{0,1:T(8,128)} collective-permute-done((f32[3072,128]{0,1:T(8,128)S(1)}, f32[3072,128]{0,1:T(8,128)}, u32[]{:S(2)}, u32[]{:S(2)}) %collective-permute-start.5) | collective-permute-done | bytes 1572896 | tf_op jit(solution)/shard_map/ppermute | solution.py:90
  297.0 31.7 %collective-permute-done.6 = f32[3072,128]{0,1:T(8,128)} collective-permute-done((f32[3072,128]{0,1:T(8,128)}, f32[3072,128]{0,1:T(8,128)}, u32[]{:S(2)}, u32[]{:S(2)}) %collective-permute-start.6) | collective-permute-done | bytes 1572896 | tf_op jit(solution)/shard_map/ppermute | solution.py:90
  355.6 11.0 %constant_dynamic-slice_fusion = f32[3072,1024]{0,1:T(8,128)} fusion(f32[3072,2048]{0,1:T(8,128)} %constant_dynamic-update-slice_fusion, s32[]{:T(128)S(6)} %select_n.148), kind=kLoop, calls=%fused_computation.118 | loop fusion | bytes 25165828 | tf_op jit(solution)/shard_map/jit(_roll_dynamic)/dynamic_slice | solution.py:93
  366.6 16.6 %gather_fusion.2 = f32[1024,3072]{1,0:T(8,128)} fusion(f32[3072,1024]{0,1:T(8,128)} %constant_dynamic-slice_fusion, s32[1024]{0:T(1024)S(1)} %broadcast_clamp_fusion), kind=kCustom, calls=%fused_computation.5 | custom fusion | bytes 25169920 | tf_op jit(solution)/shard_map/jit(_take)/gather | solution.py:94
  383.2 12.6 %copy.34 = f32[1024,3072]{0,1:T(8,128)} copy(f32[1024,3072]{1,0:T(8,128)} %gather_fusion.2) | data formatting | bytes 25165824 | tf_op jit(solution)/shard_map/jit(_take)/gather | solution.py:94
  395.8 12.4 %select_bitcast_fusion = f32[3072,1024]{1,0:T(8,128)} fusion(f32[1024,3072]{0,1:T(8,128)} %copy.34, pred[1024]{0:T(1024)(128)(4,1)S(1)} %compare_and_fusion.2), kind=kLoop, calls=%fused_computation.9 | loop fusion | flops 3145728 | bytes 25166848 | tf_op jit(solution)/shard_map/jit(_take)/select_n | solution.py:94
  408.2 4.9 fusion
  413.1 3.7 fusion.40
  419.1 5.3 gather_fusion.3
  426.1 5.4 multiply_add_fusion.3
  433.2 26.4 %all-reduce.14.cloned.1.call-done = f32[1024,256]{1,0:T(8,128)} async-done(((f32[1024,256]{1,0:T(8,128)}), f32[1024,256]{1,0:T(8,128)}) %all-reduce.14.cloned.1.call-update) | async-done | bytes 1048592 | tf_op jit(solution)/shard_map/psum | solution.py:124
  459.6 7.3 convolution_subtract_fusion.5
  466.9 4.1 fusion.13
  472.6 3.4 fusion.39
  476.0 3.5 copy.36
  479.6 6.5 gather_fusion.4
  489.1 7.0 multiply_add_fusion.2
  496.1 8.0 convolution_subtract_fusion.4
  505.8 8.0 convolution_subtract_fusion.2
  513.8 11.8 %all-reduce.16.cloned.1.call-done = f32[1024,256]{1,0:T(8,128)} async-done(((f32[1024,256]{1,0:T(8,128)}), f32[1024,256]{1,0:T(8,128)}) %all-reduce.16.cloned.1.call-update) | async-done | bytes 1048592 | tf_op jit(solution)/shard_map/psum | solution.py:124
  525.6 8.3 %convolution_subtract_fusion.3 = f32[3072,256]{1,0:T(8,128)S(1)} fusion(f32[3072,256]{1,0:T(8,128)} %convolution_subtract_fusion.4, f32[3072,256]{0,1:T(8,128)} %multiply_add_fusion.2, f32[1024,256]{1,0:T(8,128)} %all-reduce.16.cloned.1.call-done), kind=kOutput, calls=%fused_computation.15 | convolution fusion | flops 2416705536 | bytes 9699328 | tf_op jit(solution)/shard_map/dot_general | solution.py:100
  533.9 4.1 fusion.11
  543.0 3.5 copy.37
  546.5 6.5 gather_fusion.5
  556.0 7.0 multiply_add_fusion.1
  565.5 8.1 convolution_subtract_fusion.1
  573.6 19.0 %all-reduce.18.cloned.1.call-done = f32[1024,256]{1,0:T(8,128)} async-done(((f32[1024,256]{1,0:T(8,128)}), f32[1024,256]{1,0:T(8,128)}) %all-reduce.18.cloned.1.call-update) | async-done | bytes 1048592 | tf_op jit(solution)/shard_map/psum | solution.py:124
  592.6 8.3 %convolution_subtract_fusion = f32[3072,256]{1,0:T(8,128)S(1)} fusion(f32[3072,256]{1,0:T(8,128)} %convolution_subtract_fusion.1, f32[3072,256]{0,1:T(8,128)} %multiply_add_fusion.1, f32[1024,256]{1,0:T(8,128)} %all-reduce.18.cloned.1.call-done), kind=kOutput, calls=%fused_computation.12 | convolution fusion | flops 2416705536 | bytes 9699328 | tf_op jit(solution)/shard_map/dot_general | solution.py:100
  600.9 4.5 fusion.9
  612.4 4.4 fusion.37
  621.3 5.2 pad_maximum_fusion
  626.5 12.7 %copy.38 = f32[3072,1024]{1,0:T(8,128)} copy(f32[3072,1024]{0,1:T(8,128)} %pad_maximum_fusion) | data formatting | bytes 25165824
  639.2 89.8 %all-reduce.20.cloned.1.call-done = (f32[1536,256]{0,1:T(8,128)}, f32[1536,256]{0,1:T(8,128)}, f32[1536,256]{0,1:T(8,128)}, f32[1536,256]{0,1:T(8,128)}) async-done(((f32[1536,256]{0,1:T(8,128)}, f32[1536,256]{0,1:T(8,128)}, f32[1536,256]{0,1:T(8,128)}, f32[1536,256]{0,1:T(8,128)}), (f32[1536,256]{0,1:T(8,128)}, f32[1536,256]{0,1:T(8,128)}, f32[1536,256]{0,1:T(8,128)}, ...) | async-done | bytes 6291472 | tf_op jit(solution)/shard_map/psum | solution.py:12
  729.0 19.9 %fusion.44 = f32[3072,1536]{1,0:T(8,128)} fusion(f32[3072,256]{0,1:T(8,128)} %multiply_add_fusion.1, f32[1536,256]{0,1:T(8,128)} %get-tuple-element.11), kind=kOutput, calls=%fused_computation.136 | convolution fusion | flops 14495514624 | bytes 23592960 | tf_op jit(solution)/shard_map/dot_general | solution.py:118
  748.9 18.3 %fusion.43 = f32[3072,1536]{1,0:T(8,128)} fusion(f32[3072,256]{0,1:T(8,128)S(1)} %copy-done.10, f32[1536,256]{0,1:T(8,128)S(1)} %copy-done.26), kind=kOutput, calls=%fused_computation.135 | convolution fusion | flops 14495514624 | bytes 23592960 | tf_op jit(solution)/shard_map/dot_general | solution.py:118
  767.2 18.0 %fusion.42 = f32[3072,1536]{1,0:T(8,128)} fusion(f32[3072,256]{0,1:T(8,128)S(1)} %multiply_add_fusion.3, f32[1536,256]{0,1:T(8,128)S(1)} %copy-done.25), kind=kOutput, calls=%fused_computation.134 | convolution fusion | flops 14495514624 | bytes 23592960 | tf_op jit(solution)/shard_map/dot_general | solution.py:118
  785.1 38.2 %subtract_select_fusion = f32[3072,1536]{1,0:T(8,128)} fusion(f32[3072,1536]{1,0:T(8,128)} %fusion.44, f32[3072,1536]{1,0:T(8,128)} %fusion.43, f32[3072,1536]{1,0:T(8,128)} %convolution_add_fusion, f32[3072,1536]{1,0:T(8,128)} %fusion.42, f32[3072,256]{0,1:T(8,128)} %copy-done.15, f32[1536,256]{0,1:T(8,128)} %get-tuple-element.14, ...), kind=kOutput, calls=%fused_computation.6 | convolution fusion | flops 14523826176 | bytes 99095040 | tf_op jit(solution)/shard_map/dot_general | solution.py:118
  (145 shorter events, 77.4 us)
Async XLA Ops:
  7.2 9.3 %copy-start = (f32[8,3072]{1,0:T(8,128)S(1)}, f32[8,3072]{1,0:T(8,128)}, u32[]{:S(2)}) copy-start(f32[8,3072]{1,0:T(8,128)} %param.11) | copy-start | bytes 294916
  9.2 13.7 %all-to-all-start.1 = ((s32[8,1,2]{2,1,0:T(1,128)}), s32[8,1,2]{2,1,0:T(1,128)S(1)}, u32[]{:S(2)}, u32[]{:S(2)}) async-start(s32[8,1,2]{2,1,0:T(1,128)} %copy.32), calls=%async_computation.1 | async-start | bytes 8192 | tf_op jit(solution)/shard_map/all_to_all | solution.py:63
  22.9 13.8 %all-to-all-start = ((f32[8,2,3072]{2,1,0:T(2,128)}), f32[8,2,3072]{2,1,0:T(2,128)S(1)}, u32[]{:S(2)}, u32[]{:S(2)}) async-start(f32[8,2,3072]{2,1,0:T(2,128)} %copy.31), calls=%async_computation | async-start | bytes 393216 | tf_op jit(solution)/shard_map/all_to_all | solution.py:62
  28.9 430.7 %all-reduce.14.cloned.1.call-start = ((), (), s32[]{:S(2)}) async-start(), calls=%async_computation.2 | async-start | bytes 2097152 | tf_op jit(solution)/shard_map/psum | solution.py:124
  81.7 215.1 %copy-start.28 = (f32[1024]{0:T(1024)S(1)}, f32[1024]{0:T(1024)}, u32[]{:S(2)}) copy-start(f32[1024]{0:T(1024)} %param.17) | copy-start | bytes 12292
  81.7 215.1 %copy-start.29 = (s32[1024]{0:T(1024)S(1)}, s32[1024]{0:T(1024)}, u32[]{:S(2)}) copy-start(s32[1024]{0:T(1024)} %param.14) | copy-start | bytes 12292
  81.7 215.2 %copy-start.30 = (f32[1024]{0:T(1024)S(1)}, f32[1024]{0:T(1024)}, u32[]{:S(2)}) copy-start(f32[1024]{0:T(1024)} %param.16) | copy-start | bytes 12292
  82.0 36.9 %collective-permute-start = (f32[3072,128]{0,1:T(8,128)S(1)}, f32[3072,128]{0,1:T(8,128)S(1)}, u32[]{:S(2)}, u32[]{:S(2)}) collective-permute-start(f32[3072,128]{0,1:T(8,128)S(1)} %select_bitcast_fusion.1), channel_id=1, source_target_pairs={{0,1},{1,2},{2,3},{3,4},{4,5},{5,6},{6,7},{7,0},{8,9},{9,10},{10,1... | collective-permute-start | bytes 4718600 | tf_op jit(solution)/shard_map/ppermute | solution.py:90
  118.9 36.0 %collective-permute-start.1 = (f32[3072,128]{0,1:T(8,128)S(1)}, f32[3072,128]{0,1:T(8,128)S(1)}, u32[]{:S(2)}, u32[]{:S(2)}) collective-permute-start(f32[3072,128]{0,1:T(8,128)S(1)} %collective-permute-done), channel_id=1, source_target_pairs={{0,1},{1,2},{2,3},{3,4},{4,5},{5,6},{6,7},{7,0},{8,9},{9,10},{10,1... | collective-permute-start | bytes 4718600 | tf_op jit(solution)/shard_map/ppermute | solution.py:90
  154.9 1.2 copy-start.17
  156.1 35.1 %collective-permute-start.2 = (f32[3072,128]{0,1:T(8,128)S(1)}, f32[3072,128]{0,1:T(8,128)S(1)}, u32[]{:S(2)}, u32[]{:S(2)}) collective-permute-start(f32[3072,128]{0,1:T(8,128)S(1)} %collective-permute-done.1), channel_id=1, source_target_pairs={{0,1},{1,2},{2,3},{3,4},{4,5},{5,6},{6,7},{7,0},{8,9},{9,10},{10,1... | collective-permute-start | bytes 4718600 | tf_op jit(solution)/shard_map/ppermute | solution.py:90
  191.2 1.1 copy-start.19
  192.4 34.3 %collective-permute-start.3 = (f32[3072,128]{0,1:T(8,128)S(1)}, f32[3072,128]{0,1:T(8,128)S(1)}, u32[]{:S(2)}, u32[]{:S(2)}) collective-permute-start(f32[3072,128]{0,1:T(8,128)S(1)} %collective-permute-done.2), channel_id=1, source_target_pairs={{0,1},{1,2},{2,3},{3,4},{4,5},{5,6},{6,7},{7,0},{8,9},{9,10},{10,1... | collective-permute-start | bytes 4718600 | tf_op jit(solution)/shard_map/ppermute | solution.py:90
  226.6 1.1 copy-start.21
  227.8 33.4 %collective-permute-start.4 = (f32[3072,128]{0,1:T(8,128)S(1)}, f32[3072,128]{0,1:T(8,128)S(1)}, u32[]{:S(2)}, u32[]{:S(2)}) collective-permute-start(f32[3072,128]{0,1:T(8,128)S(1)} %collective-permute-done.3), channel_id=1, source_target_pairs={{0,1},{1,2},{2,3},{3,4},{4,5},{5,6},{6,7},{7,0},{8,9},{9,10},{10,1... | collective-permute-start | bytes 4718600 | tf_op jit(solution)/shard_map/ppermute | solution.py:90
  261.2 1.1 copy-start.23
  262.3 34.2 %collective-permute-start.5 = (f32[3072,128]{0,1:T(8,128)S(1)}, f32[3072,128]{0,1:T(8,128)}, u32[]{:S(2)}, u32[]{:S(2)}) collective-permute-start(f32[3072,128]{0,1:T(8,128)S(1)} %collective-permute-done.4), channel_id=1, source_target_pairs={{0,1},{1,2},{2,3},{3,4},{4,5},{5,6},{6,7},{7,0},{8,9},{9,10},{10,1... | collective-permute-start | bytes 4718600 | tf_op jit(solution)/shard_map/ppermute | solution.py:90
  296.5 32.2 %collective-permute-start.6 = (f32[3072,128]{0,1:T(8,128)}, f32[3072,128]{0,1:T(8,128)}, u32[]{:S(2)}, u32[]{:S(2)}) collective-permute-start(f32[3072,128]{0,1:T(8,128)} %collective-permute-done.5), channel_id=1, source_target_pairs={{0,1},{1,2},{2,3},{3,4},{4,5},{5,6},{6,7},{7,0},{8,9},{9,10},{10,1... | collective-permute-start | bytes 4718600 | tf_op jit(solution)/shard_map/ppermute | solution.py:90
  297.0 37.2 %copy-start.24 = (f32[3072,128]{0,1:T(8,128)S(1)}, f32[3072,128]{0,1:T(8,128)}, u32[]{:S(2)}) copy-start(f32[3072,128]{0,1:T(8,128)} %copy-done.23) | copy-start | bytes 4718596
  331.4 4.1 copy-start.22
  334.2 2.6 copy-start.20
  335.6 2.6 copy-start.18
  413.0 3.7 copy-start.4
  425.8 99.7 %all-reduce.16.cloned.1.call-start = ((), (), s32[]{:S(2)}) async-start(), calls=%async_computation.3 | async-start | bytes 2097152 | tf_op jit(solution)/shard_map/psum | solution.py:124
  426.1 5.4 copy-start.5
  471.0 1.6 copy-start.6
  488.7 103.9 %all-reduce.18.cloned.1.call-start = ((), (), s32[]{:S(2)}) async-start(), calls=%async_computation.4 | async-start | bytes 2097152 | tf_op jit(solution)/shard_map/psum | solution.py:124
  489.1 7.0 copy-start.27
  496.1 8.0 copy-start.7
  538.0 1.7 copy-start.2
  555.7 173.3 %all-reduce.20.cloned.1.call-start = ((), (), s32[]{:S(2)}) async-start(), calls=%async_computation.5 | async-start | bytes 12582912 | tf_op jit(solution)/shard_map/psum | solution.py:12
  555.9 7.1 copy-start.3
  556.0 8.7 %copy-start.16 = (f32[3072,256]{1,0:T(8,128)S(1)}, f32[3072,256]{1,0:T(8,128)}, u32[]{:S(2)}) copy-start(f32[3072,256]{1,0:T(8,128)} %convolution_subtract_fusion.2) | copy-start | bytes 9437188
  563.0 2.5 copy-start.8
  605.4 1.7 copy-start.12
  608.7 0.7 copy-start.11
  612.4 4.9 copy-start.13
  617.3 3.0 copy-start.9
  617.3 4.0 copy-start.14
  618.6 1.7 copy-start.15
  729.0 19.9 %copy-start.10 = (f32[3072,256]{0,1:T(8,128)S(1)}, f32[3072,256]{0,1:T(8,128)}, u32[]{:S(2)}) copy-start(f32[3072,256]{0,1:T(8,128)} %multiply_add_fusion.2) | copy-start | bytes 9437188
  729.0 19.9 %copy-start.26 = (f32[1536,256]{0,1:T(8,128)S(1)}, f32[1536,256]{0,1:T(8,128)}, u32[]{:S(2)}) copy-start(f32[1536,256]{0,1:T(8,128)} %get-tuple-element.12) | copy-start | bytes 4718596
  748.9 18.3 %copy-start.25 = (f32[1536,256]{0,1:T(8,128)S(1)}, f32[1536,256]{0,1:T(8,128)}, u32[]{:S(2)}) copy-start(f32[1536,256]{0,1:T(8,128)} %get-tuple-element.13) | copy-start | bytes 4718596
  785.1 38.2 %copy-start.1 = (f32[8,3072]{1,0:T(8,128)S(1)}, f32[8,3072]{1,0:T(8,128)}, u32[]{:S(2)}) copy-start(f32[8,3072]{1,0:T(8,128)} %param.11) | copy-start | bytes 294916
Sparse Core Ops, SparseCore 0:
  426.0 33.5 all-reduce.13
  488.8 36.7 all-reduce.15
  555.8 36.7 all-reduce.17
  608.9 120.0 all-reduce.19
